TPU v7x, 32 devices: a whole 2x2x4 slice. The times are simulated.
32 devices in a mesh: grp: 8 (over y, x, core), seq: 4 (over z).
Axes of the slice: x: 2, y: 2, z: 4, core: 2. Of those that a mesh axis runs over, the one named last changes fastest.
Arguments:
- tokens: bfloat16 [8192, 512], P(('grp', 'seq')), parts along dimension 0, may hold values from -6 to 6
- group_pos: int32 [2048], P('grp'), parts along dimension 0, may hold values from 0 to 1023, as said below
- log_decay: float32 [8192, 16], P(('grp', 'seq')), parts along dimension 0, may hold values from -1 to 0, as said below
- in_weight: bfloat16 [512, 2176], replicated, may hold values from -0.25 to 0.25
- norm_gain: float32 [1024], replicated, may hold values from 0.1 to 1.9
- out_weight: bfloat16 [1024, 512], replicated, may hold values from -0.1875 to 0.1875
- inner_gain: float32 [512], replicated, may hold values from 0.1 to 1.9
- qkv_weight: bfloat16 [4, 512, 192], P('seq'), may hold values from -1 to 1
- attn_out: bfloat16 [4, 64, 512], P('seq'), may hold values from -0.375 to 0.375
Outputs:
- result: bfloat16 [8192, 512], P(('grp', 'seq')), parts along dimension 0
There are 8 independent parts, one for each index of `grp`. A program takes and returns all parts, laid end to end along the dimension named above; an argument that names none is the same for every part. Nothing has to cross between parts.
Inputs may be any that keep to these rules, and one draw needn't show every extreme that they name: `group_pos`: strictly increasing. Each device's 256 positions hold at least one group start and at most 128; some device holds exactly 128. `log_decay`: negative at every position.
All inputs are finite; a program needn't handle non-finite values.
Results may differ from a plain program's by a relative error of at most 0.0061.
Values may be sent and summed in bfloat16 or wider, within the bound.
No kernel may reach another device: no remote copies, remote signals or barrier semaphores. Data moves between devices by JAX's collectives and lax.ppermute only.
A program may use at most 64 MiB of HBM per device.

v0:
```python
import jax
import jax.numpy as jnp
from jax import lax
from jax.sharding import PartitionSpec as P


def entering(value, axis, join, neutral):
    count, mine = (lax.axis_size(axis), lax.axis_index(axis))
    pieces = jax.tree.map(lambda part: lax.all_gather(part, axis), value)
    subtotal = jax.tree.map(
        lambda part, zero: jnp.full_like(part, 0) + jnp.asarray(zero, part.dtype), value, neutral
    )

    def turn(position, subtotal):
        longer = join(subtotal, jax.tree.map(lambda part: part[position], pieces))
        return jax.tree.map(lambda new, old: jnp.where(position < mine, new, old), longer, subtotal)

    return lax.fori_loop(0, count - 1, turn, subtotal)


def rms_norm(values, gain):
    return values * lax.rsqrt(jnp.mean(values * values, axis=-1, keepdims=True) + 1e-05) * gain


def attend(rows, w_qkv, index, valid):
    head_dim = w_qkv.shape[1] // 3
    qkv = jnp.dot(rows, w_qkv, preferred_element_type=jnp.float32).astype(jnp.bfloat16)
    query = qkv[:, :head_dim]
    keys = qkv[:, head_dim : 2 * head_dim]
    values = qkv[:, 2 * head_dim :]
    count = rows.shape[0]
    block = min(512, count)

    def one_block(start):
        query_block = lax.dynamic_slice_in_dim(query, start, block, 0)
        index_block = lax.dynamic_slice_in_dim(index, start, block, 0)
        scores = jnp.dot(query_block, keys.T, preferred_element_type=jnp.float32) * head_dim ** (
            -0.5
        )
        allowed = (index[None, :] <= index_block[:, None]) & valid[None, :]
        scores = jnp.where(allowed, scores, -jnp.inf)
        top = jnp.max(scores, axis=1, keepdims=True)
        expo = jnp.exp(scores - top)
        probs = (expo / jnp.sum(expo, axis=1, keepdims=True)).astype(jnp.bfloat16)
        return jnp.dot(probs, values, preferred_element_type=jnp.float32).astype(jnp.bfloat16)

    starts = jnp.arange(count // block, dtype=jnp.int32) * block
    return lax.map(one_block, starts).reshape(count, head_dim)


def shards(
    tokens, group_pos, log_decay, in_weight, norm_gain, out_weight, inner_gain, qkv_weight, attn_out
):
    highest = lax.Precision.HIGHEST
    length = tokens.shape[0]
    heads = log_decay.shape[1]
    width = out_weight.shape[0]
    model_width = out_weight.shape[1]
    head_size = width // heads
    state_dim = (in_weight.shape[1] - 2 * width) // 2
    proj = jnp.dot(tokens, in_weight, preferred_element_type=jnp.float32).astype(jnp.bfloat16)
    xs = proj[:, :width].astype(jnp.float32).reshape(length, heads, head_size)
    gate = proj[:, width : 2 * width].astype(jnp.float32)
    bmat = proj[:, 2 * width : 2 * width + state_dim].astype(jnp.float32)
    cmat = proj[:, 2 * width + state_dim :].astype(jnp.float32)
    cumul = jnp.cumsum(log_decay, axis=0)
    differ = cumul.T[:, :, None] - cumul.T[:, None, :]
    lower = jnp.arange(length)[:, None] >= jnp.arange(length)[None, :]
    decays = jnp.exp(jnp.where(lower[None], differ, -jnp.inf))
    intersections = jnp.dot(cmat, bmat.T, precision=highest)
    within = jnp.einsum("hij,jhp->ihp", decays * intersections[None], xs, precision=highest)
    tails = jnp.exp(cumul[-1][None, :] - cumul)
    local_state = jnp.einsum("jh,jhp,jn->hpn", tails, xs, bmat, precision=highest)
    total_decay = jnp.exp(cumul[-1])

    def link(earlier, later):
        return (earlier[0] * later[0], later[0][:, None, None] * earlier[1] + later[1])

    identity = (jnp.ones_like(total_decay), jnp.zeros_like(local_state))
    _, state_in = entering((total_decay, local_state), "seq", link, identity)
    carried = jnp.einsum("ih,in,hpn->ihp", jnp.exp(cumul), cmat, state_in, precision=highest)
    gated = (within + carried).reshape(length, width) * jax.nn.silu(gate)
    normed = rms_norm(gated, norm_gain).astype(jnp.bfloat16)
    hidden = (
        tokens.astype(jnp.float32) + jnp.dot(normed, out_weight, preferred_element_type=jnp.float32)
    ).astype(jnp.bfloat16)
    position = lax.axis_index("seq")
    devices = lax.axis_size("seq")
    most = length // 2
    groups = group_pos.shape[0]
    starts = jnp.arange(devices, dtype=jnp.int32) * length
    before = jnp.sum((group_pos[None, :] < starts[:, None]).astype(jnp.int32), axis=1)
    upto = jnp.sum((group_pos[None, :] < (starts + length)[:, None]).astype(jnp.int32), axis=1)
    counts = upto - before
    slots = jnp.arange(most, dtype=jnp.int32)
    picks = jnp.clip(before[position] + slots, 0, groups - 1)
    valid_here = slots < counts[position]
    local_pos = group_pos[picks] - position * length
    placing = (
        (local_pos[:, None] == jnp.arange(length, dtype=jnp.int32)[None, :]) & valid_here[:, None]
    ).astype(jnp.float32)
    rows = jnp.dot(placing.astype(jnp.bfloat16), hidden, preferred_element_type=jnp.float32)
    rows_n = rms_norm(rows, inner_gain).astype(jnp.bfloat16)
    gathered = lax.all_gather(rows_n, "seq", axis=0, tiled=True)
    slot_group = (before[:, None] + slots[None, :]).reshape(-1)
    slot_valid = (slots[None, :] < counts[:, None]).reshape(-1)
    w_qkv = qkv_weight[0]
    heads_out = attend(gathered, w_qkv, slot_group, slot_valid)
    full_out = lax.all_gather(attn_out, "seq", axis=0, tiled=True)
    mine = lax.all_to_all(heads_out[:, None, :], "seq", split_axis=0, concat_axis=1, tiled=True)
    back = jnp.dot(
        mine.reshape(most, -1),
        full_out.reshape(-1, model_width),
        preferred_element_type=jnp.float32,
    )
    placed = jnp.dot(placing.T, back, precision=highest)
    return (hidden.astype(jnp.float32) + placed).astype(jnp.bfloat16)


def solution(mesh):
    in_specs = (
        P(("grp", "seq"), None),
        P("grp"),
        P(("grp", "seq"), None),
        P(),
        P(),
        P(),
        P(),
        P("seq", None, None),
        P("seq", None, None),
    )
    out_specs = P(("grp", "seq"), None)
    return jax.shard_map(shards, mesh=mesh, in_specs=in_specs, out_specs=out_specs, check_vma=False)
```

profile of v0, /device:TPU:0, one launch (start us, length us, event | category | flops | bytes accessed | tf_op | source)
XLA Modules:
  0.0 115.9 jit_solution(2016591434502746078)
XLA Ops:
  6.5 0.9 copy_bitcast_fusion.1
  7.4 0.6 reduce-window.6
  8.0 0.2 slice_reduce_fusion
  8.2 0.1 fusion.52
  8.3 0.2 slice_reduce_fusion.1
  8.5 0.1 bitcast_exponential_fusion
  8.6 1.9 %convolution_convert_fusion = bf16[256,2176]{0,1:T(8,128)(2,1)S(1)} fusion(bf16[256,512]{1,0:T(8,128)(2,1)} %param.11, bf16[512,2176]{1,0:T(8,128)(2,1)S(1)} %copy-done), kind=kOutput, calls=%fused_computation.9 | convolution fusion | flops 570982400 | bytes 3604480 | tf_op jit(solution)/shard_map/dot_general | solution.py:61
  10.6 1.0 copy-done.2
  11.5 1.5 %fusion.23 = f32[16,64,64]{2,1,0:T(8,128)} fusion(bf16[256,16,64]{0,2,1:T(8,128)(2,1)S(1)} %bitcast.77, f32[256,16]{0,1:T(8,128)S(1)} %get-tuple-element.159, bf16[256,2176]{0,1:T(8,128)(2,1)S(1)} %convolution_convert_fusion), kind=kOutput, calls=%fused_computation.37 | convolution fusion | flops 201850880 | bytes 835584 | tf_op jit(solution)/shard_map/jh,jhp,jn->hpn/dot_general | solution.py:73
  13.0 0.0 all-gather.4.cloned.1.call-update
  13.0 0.2 convert_reduce_fusion
  13.2 0.6 dynamic_slice.27
  13.8 0.7 fusion.50
  14.5 0.6 dynamic_slice.28
  15.1 0.6 iota_compare_fusion.3
  15.8 1.3 %gather_fusion = s32[128]{0:T(128)S(1)} fusion(s32[256]{0:T(256)S(1)} %copy-done.1, s32[1024]{0:T(1024)S(1)} %pad_clamp_fusion), kind=kCustom, calls=%fused_computation | custom fusion | bytes 1536 | tf_op jit(solution)/shard_map/gather | solution.py:98
  17.1 12.7 %all-gather.1 = f32[4,1,16]{2,1,0:T(1,128)S(1)} all-gather(f32[1,1,16]{2,1,0:T(1,128)S(1)} %bitcast.82), channel_id=1, replica_groups=mesh['grp'=8,'seq'=4] {'seq'}, dimensions={0}, use_global_device_ids=true | all-gather | bytes 320 | tf_op jit(solution)/shard_map/all_gather | solution.py:9
  29.8 0.1 fusion.49
  29.8 0.1 add_bitcast_fusion.1
  29.9 0.8 slice_convert_fusion
  30.7 1.0 fusion.46
  31.7 4.1 %fusion.11 = f32[256,16,64]{0,2,1:T(8,128)} fusion(bf16[256,16,64]{0,2,1:T(8,128)(2,1)S(1)} %bitcast.78, f32[256,256]{1,0:T(8,128)S(1)} %fusion.46, f32[16,256]{1,0:T(8,128)S(1)} %get-tuple-element.161, pred[256,256]{1,0:T(8,128)(4,1)S(1)} %iota_compare_fusion), kind=kOutput, calls=%fused_computation.15 | convolution fusion | flops 808452096 | bytes 1916928 | tf_op jit(solution)/shard_map/hij,jhp->ihp/dot_general | solution.py:71
  35.7 25.8 %all-gather.4.cloned.1.call-done = f32[64,64,64]{2,1,0:T(8,128)} async-done(((f32[16,64,64]{2,1,0:T(8,128)}), f32[64,64,64]{2,1,0:T(8,128)}) %all-gather.4.cloned.1.call-update) | async-done | bytes 1048592 | tf_op jit(solution)/shard_map/all_gather | solution.py:9
  61.6 3.6 %while.18 = (s32[]{:T(128)}, f32[16,64,64]{2,1,0:T(8,128)S(1)}, s32[]{:T(128)}, f32[4,16]{1,0:T(4,128)S(1)}, f32[4,16,64,64]{3,2,1,0:T(8,128)}, /*index=5*/s32[]{:T(128)}, s32[]{:T(128)}) while((s32[]{:T(128)}, f32[16,64,64]{2,1,0:T(8,128)S(1)}, s32[]{:T(128)}, f32[4,16]{1,0:T(4,128)S(1)}, f32[4,16,64,64]{3,2,1,0:T(8,128)}, ...), condition=%wide.region_3.4_spmd.clone, body=%wide.region_2.3_spmd.clone.sunk | while | flops 262148 | bytes 786729 | solution.py:18
  61.6 1.2 %fusion.68 = f32[16,64,64]{2,1,0:T(8,128)S(1)} fusion(f32[4,16,64,64]{3,2,1,0:T(8,128)} %get-tuple-element.217, s32[]{:T(128)} %get-tuple-element.206, f32[16,64,64]{2,1,0:T(8,128)S(1)} %get-tuple-element.207, f32[16]{0:T(128)S(1)} %dynamic-slice_bitcast_fusion.2, pred[]{:T(512)S(6)} %compare.3, pred[]{:T(512)S(6)} %lt.120), kind=kLoop, calls=%fused_computation.2.clone.1 | loop fusion | flops 262144 | bytes 786502 | tf_op jit(solution)/shard_map/while/body/eval_jaxpr/jit(_where)/select_n | solution.py:16
  62.8 1.2 %fusion.68 = f32[16,64,64]{2,1,0:T(8,128)S(1)} fusion(f32[4,16,64,64]{3,2,1,0:T(8,128)} %get-tuple-element.217, s32[]{:T(128)} %get-tuple-element.206, f32[16,64,64]{2,1,0:T(8,128)S(1)} %get-tuple-element.207, f32[16]{0:T(128)S(1)} %dynamic-slice_bitcast_fusion.2, pred[]{:T(512)S(6)} %compare.3, pred[]{:T(512)S(6)} %lt.120), kind=kLoop, calls=%fused_computation.2.clone.1 | loop fusion | flops 262144 | bytes 786502 | tf_op jit(solution)/shard_map/while/body/eval_jaxpr/jit(_where)/select_n | solution.py:16
  64.0 1.2 %fusion.68 = f32[16,64,64]{2,1,0:T(8,128)S(1)} fusion(f32[4,16,64,64]{3,2,1,0:T(8,128)} %get-tuple-element.217, s32[]{:T(128)} %get-tuple-element.206, f32[16,64,64]{2,1,0:T(8,128)S(1)} %get-tuple-element.207, f32[16]{0:T(128)S(1)} %dynamic-slice_bitcast_fusion.2, pred[]{:T(512)S(6)} %compare.3, pred[]{:T(512)S(6)} %lt.120), kind=kLoop, calls=%fused_computation.2.clone.1 | loop fusion | flops 262144 | bytes 786502 | tf_op jit(solution)/shard_map/while/body/eval_jaxpr/jit(_where)/select_n | solution.py:16
  65.2 0.0 copy-start.4
  65.2 2.4 %fusion.15 = f32[256,16,64]{0,2,1:T(8,128)S(1)} fusion(f32[256,16,64]{0,2,1:T(8,128)} %fusion.11, f32[16,64,64]{2,1,0:T(8,128)S(1)} %get-tuple-element.123, f32[256,16]{0,1:T(8,128)S(1)} %get-tuple-element.158, f32[256,64]{0,1:T(8,128)S(1)} %slice_convert_fusion), kind=kOutput, calls=%fused_computation.19 | convolution fusion | flops 201850880 | bytes 2441216 | tf_op jit(solution)/shard_map/ih,in,hpn->ihp/dot_general | solution.py:81
  67.6 1.4 %multiply_reduce_fusion = (f32[256]{0:T(256)S(1)}, f32[256,1024]{0,1:T(8,128)S(1)}) fusion(bf16[256,2176]{0,1:T(8,128)(2,1)} %copy-done.2, f32[256,16,64]{0,2,1:T(8,128)S(1)} %fusion.15), kind=kLoop, calls=%fused_computation.36 | loop fusion | flops 2096896 | bytes 2622464 | tf_op jit(solution)/shard_map/reduce_sum | solution.py:22
  69.1 0.8 fusion.16
  69.9 0.3 multiply_reduce_fusion.1
  70.2 0.1 multiply_convert_fusion.2
  70.3 15.6 %all_gather.19 = bf16[512,512]{1,0:T(8,128)(2,1)S(1)} all-gather(bf16[128,512]{1,0:T(8,128)(2,1)S(1)} %multiply_convert_fusion.2), channel_id=1, replica_groups=mesh['grp'=8,'seq'=4] {'seq'}, dimensions={0}, use_global_device_ids=true | all-gather | bytes 655360 | tf_op jit(solution)/shard_map/all_gather | solution.py:104
  85.9 0.3 convolution_convert_fusion.1
  86.3 0.5 fusion.54
  86.7 0.2 fusion.27
  86.9 0.3 fusion.18
  87.2 0.5 broadcast.142
  87.8 0.7 reduce.6
  88.4 0.1 copy.76
  88.6 0.8 reshape.183
  89.4 3.3 %all-to-all-start = ((bf16[4,2,4096]{2,1,0:T(2,128)(2,1)}), bf16[4,2,4096]{2,1,0:T(2,128)(2,1)S(1)}, u32[]{:S(2)}, u32[]{:S(2)}) async-start(bf16[4,2,4096]{2,1,0:T(2,128)(2,1)} %reshape.183), calls=%async_computation | async-start | bytes 131072 | tf_op jit(solution)/shard_map/all_to_all | solution.py:110
  92.7 14.6 %all_gather.20 = bf16[4,64,512]{2,1,0:T(8,128)(2,1)S(1)} all-gather(bf16[1,64,512]{2,1,0:T(8,128)(2,1)S(1)} %copy-done.6), channel_id=1, replica_groups=mesh['grp'=8,'seq'=4] {'seq'}, dimensions={0}, use_global_device_ids=true | all-gather | bytes 327680 | tf_op jit(solution)/shard_map/all_gather | solution.py:109
  107.3 0.1 reshape.184
  107.4 0.1 copy.63
  107.6 0.2 fusion.55
  107.8 1.2 %fusion.17 = bf16[256,512]{1,0:T(8,128)(2,1)} fusion(f32[128,512]{1,0:T(8,128)S(1)} %fusion.55, bf16[256,512]{1,0:T(8,128)(2,1)S(1)} %fusion.16, s32[128]{0:T(128)S(1)} %broadcast_subtract_fusion, pred[128]{0:T(512)(128)(4,1)S(1)} %iota_compare_fusion.3), kind=kOutput, calls=%fused_computation.25 | convolution fusion | flops 201785344 | bytes 787072 | tf_op jit(solution)/shard_map/dot_general | solution.py:116
  (34 shorter events, 0.2 us)
Async XLA Ops:
  6.5 2.0 %copy-start = (bf16[512,2176]{1,0:T(8,128)(2,1)S(1)}, bf16[512,2176]{1,0:T(8,128)(2,1)}, u32[]{:S(2)}) copy-start(bf16[512,2176]{1,0:T(8,128)(2,1)} %param.14) | copy-start | bytes 6684676
  6.5 55.0 %all-gather.4.cloned.1.call-start = ((), (), s32[]{:S(2)}) async-start(), calls=%async_computation.1 | async-start | bytes 2621440 | tf_op jit(solution)/shard_map/all_gather | solution.py:9
  10.5 1.0 copy-start.2
  10.5 2.5 %copy-start.1 = (s32[256]{0:T(256)S(1)}, s32[256]{0:T(256)}, u32[]{:S(2)}) copy-start(s32[256]{0:T(256)} %param.12) | copy-start | bytes 3076
  65.2 3.9 %copy-start.3 = (bf16[256,512]{1,0:T(8,128)(2,1)S(1)}, bf16[256,512]{1,0:T(8,128)(2,1)}, u32[]{:S(2)}) copy-start(bf16[256,512]{1,0:T(8,128)(2,1)} %param.11) | copy-start | bytes 786436
  65.2 3.9 %copy-start.4 = (bf16[1024,512]{1,0:T(8,128)(2,1)S(1)}, bf16[1024,512]{1,0:T(8,128)(2,1)}, u32[]{:S(2)}) copy-start(bf16[1024,512]{1,0:T(8,128)(2,1)} %param.16) | copy-start | bytes 3145732
  65.2 3.9 %copy-start.7 = (f32[1024]{0:T(1024)S(1)}, f32[1024]{0:T(1024)}, u32[]{:S(2)}) copy-start(f32[1024]{0:T(1024)} %param.15) | copy-start | bytes 12292
  69.0 1.2 %copy-start.8 = (f32[512]{0:T(512)S(1)}, f32[512]{0:T(512)}, u32[]{:S(2)}) copy-start(f32[512]{0:T(512)} %param.17) | copy-start | bytes 6148
  69.0 16.9 %copy-start.5 = (bf16[1,512,192]{1,2,0:T(8,128)(2,1)S(1)}, bf16[1,512,192]{1,2,0:T(8,128)(2,1)}, u32[]{:S(2)}) copy-start(bf16[1,512,192]{1,2,0:T(8,128)(2,1)} %param.18) | copy-start | bytes 589828
  86.9 5.7 %copy-start.6 = (bf16[1,64,512]{2,1,0:T(8,128)(2,1)S(1)}, bf16[1,64,512]{2,1,0:T(8,128)(2,1)}, u32[]{:S(2)}) copy-start(bf16[1,64,512]{2,1,0:T(8,128)(2,1)} %param.19) | copy-start | bytes 196612
  89.4 17.9 %all-to-all-start = ((bf16[4,2,4096]{2,1,0:T(2,128)(2,1)}), bf16[4,2,4096]{2,1,0:T(2,128)(2,1)S(1)}, u32[]{:S(2)}, u32[]{:S(2)}) async-start(bf16[4,2,4096]{2,1,0:T(2,128)(2,1)} %reshape.183), calls=%async_computation | async-start | bytes 131072 | tf_op jit(solution)/shard_map/all_to_all | solution.py:110
Sparse Core Ops, SparseCore 0:
  13.1 48.3 all-gather.3
where the time goes:
time: 117 us; the launch traced here: 116 us
  blocking collectives  42.9 us (37%)
  waiting for transfers between devices  25.9 us (22%)
  matrix products  14.4 us (12%)
  between operations  13.7 us (12%)
  other arithmetic  9.12 us (8%)
  local copies, waits for them, and re-layouts  6.46 us (6%)
  starting transfers between devices  3.29 us (3%)
    all_gather x1, waiting for transfers between devices, entering(): pieces = jax.tree.map(lambda part: lax.all_gather(part, axis), value)  25.8 us
    all_gather x1, blocking collectives, shards(): gathered = lax.all_gather(rows_n, 'seq', axis=0, tiled=True)  15.6 us
    all_gather x1, blocking collectives, shards(): full_out = lax.all_gather(attn_out, 'seq', axis=0, tiled=True)  14.6 us
    all_gather x1, blocking collectives, entering(): pieces = jax.tree.map(lambda part: lax.all_gather(part, axis), value)  12.7 us
    dot_general x1, matrix products, shards(): jnp.einsum('hij,jhp->ihp', decays * intersections[None], xs, precision=hi...  4.07 us
    select_n x3, other arithmetic, turn(): jnp.where(position < mine, new, old)  3.51 us
    all_to_all x1, starting transfers between devices, shards(): lax.all_to_all(heads_out[:, None, :], 'seq', split_axis=0, concat_axis=1,...  3.28 us
    dot_general x1, matrix products, shards(): jnp.einsum('ih,in,hpn->ihp', jnp.exp(cumul), cmat, state_in, precision=hi...  2.42 us
  transfers between devices with their start and end apart: 2, of which 1 were waited for; matrix products, arithmetic and copies ran while one was open for 9% of the time, Pallas kernels for 0%

commit v1 on v0

--- a/solution.py
+++ b/solution.py
@@ -51,6 +51,23 @@
 def shards(
     tokens, group_pos, log_decay, in_weight, norm_gain, out_weight, inner_gain, qkv_weight, attn_out
 ):
+
+    def state_grid(mat):
+        comm_axis = "seq"
+        k_all = lax.axis_size(comm_axis)
+        pieces_in = tuple(((c, (c + 1) % k_all) for c in range(k_all)))
+
+        def do_patch(e_next):
+            if len(e_next) == k_all:
+                return e_next
+            z2 = do_patch([lax.ppermute(e_next[0], comm_axis, pieces_in), *e_next])
+            return z2
+
+        high = do_patch([mat])
+        w1 = jnp.concatenate(high, axis=0)
+        current_block = jnp.roll(w1, (lax.axis_index(comm_axis) + 1) * mat.shape[0], axis=0)
+        return current_block
+
     highest = lax.Precision.HIGHEST
     length = tokens.shape[0]
     heads = log_decay.shape[1]
@@ -106,7 +123,7 @@
     slot_valid = (slots[None, :] < counts[:, None]).reshape(-1)
     w_qkv = qkv_weight[0]
     heads_out = attend(gathered, w_qkv, slot_group, slot_valid)
-    full_out = lax.all_gather(attn_out, "seq", axis=0, tiled=True)
+    full_out = state_grid(attn_out)
     mine = lax.all_to_all(heads_out[:, None, :], "seq", split_axis=0, concat_axis=1, tiled=True)
     back = jnp.dot(
         mine.reshape(most, -1),

time: 117 us -> 111 us (0.949)
  blocking collectives: 42.9 us -> 25.8 us
  local copies, waits for them, and re-layouts: 6.46 us -> 13.1 us
  starting transfers between devices: 3.29 us -> 8.02 us
  waiting for transfers between devices: 25.9 us -> 21.9 us
  other arithmetic: 9.12 us -> 12.5 us
  matrix products: 14.4 us -> 15.8 us
    all_gather x1, waiting for transfers between devices: 25.8 us -> 10.3 us  [entering(): pieces = jax.tree.map(lambda part: lax.all_gather(part, axis), value)]
    all_gather x1 -> x0, blocking collectives: 14.6 us -> none  [shards(): full_out = lax.all_gather(attn_out, 'seq', axis=0, tiled=True)]
    ppermute x0 -> x3, waiting for transfers between devices: none -> 6.9 us  [do_patch(): z2 = do_patch([lax.ppermute(e_next[0], comm_axis, pieces_in), *e_next])]
    ppermute x0 -> x3, starting transfers between devices: none -> 4.74 us  [do_patch(): z2 = do_patch([lax.ppermute(e_next[0], comm_axis, pieces_in), *e_next])]
    all_to_all x1, waiting for transfers between devices: 0.01 us -> 4.73 us  [shards(): lax.all_to_all(heads_out[:, None, :], 'seq', split_axis=0, concat_axis=1,...]
    unnamed x21 -> x34, local copies, waits for them, and re-layouts: 2.07 us -> 6.28 us
    all_gather x1, blocking collectives: 12.7 us -> 10.2 us  [entering(): pieces = jax.tree.map(lambda part: lax.all_gather(part, axis), value)]
    dot_general x1, matrix products: 4.07 us -> 5.45 us  [shards(): jnp.einsum('hij,jhp->ihp', decays * intersections[None], xs, precision=hi...]
  transfers between devices with their start and end apart: 2 -> 5, of which waited for: 1 -> 3; matrix products, arithmetic and copies ran while one was open for 9% -> 18% of each run, Pallas kernels for 0% -> 0%
where the time goes in v1:
time: 111 us
  blocking collectives  25.8 us (23%)
  waiting for transfers between devices  21.9 us (20%)
  matrix products  15.8 us (14%)
  between operations  13.7 us (12%)
  local copies, waits for them, and re-layouts  13.1 us (12%)
  other arithmetic  12.5 us (11%)
  starting transfers between devices  8.02 us (7%)
    all_gather x1, blocking collectives, shards(): gathered = lax.all_gather(rows_n, 'seq', axis=0, tiled=True)  15.6 us
    all_gather x1, waiting for transfers between devices, entering(): pieces = jax.tree.map(lambda part: lax.all_gather(part, axis), value)  10.3 us
    all_gather x1, blocking collectives, entering(): pieces = jax.tree.map(lambda part: lax.all_gather(part, axis), value)  10.2 us
    ppermute x3, waiting for transfers between devices, do_patch(): z2 = do_patch([lax.ppermute(e_next[0], comm_axis, pieces_in), *e_next])  6.9 us
    unnamed x34, local copies, waits for them, and re-layouts  6.28 us
    dot_general x1, matrix products, shards(): jnp.einsum('hij,jhp->ihp', decays * intersections[None], xs, precision=hi...  5.45 us
    ppermute x3, starting transfers between devices, do_patch(): z2 = do_patch([lax.ppermute(e_next[0], comm_axis, pieces_in), *e_next])  4.74 us
    all_to_all x1, waiting for transfers between devices, shards(): lax.all_to_all(heads_out[:, None, :], 'seq', split_axis=0, concat_axis=1,...  4.73 us
  transfers between devices with their start and end apart: 5, of which 3 were waited for; matrix products, arithmetic and copies ran while one was open for 18% of the time, Pallas kernels for 0%

profile of v1, /device:TPU:0, one launch (start us, length us, event | category | flops | bytes accessed | tf_op | source)
XLA Modules:
  0.0 110.8 jit_solution(1094712291167799552)
XLA Ops:
  6.5 0.9 copy_bitcast_fusion.1
  7.4 0.6 reduce-window.6
  8.2 0.7 fusion.52
  9.0 0.7 bitcast_exponential_fusion
  9.7 1.9 %convolution_convert_fusion = bf16[256,2176]{0,1:T(8,128)(2,1)S(1)} fusion(bf16[256,512]{1,0:T(8,128)(2,1)} %param.11, bf16[512,2176]{1,0:T(8,128)(2,1)S(1)} %copy-done), kind=kOutput, calls=%fused_computation.9 | convolution fusion | flops 570982400 | bytes 3604480 | tf_op jit(solution)/shard_map/dot_general | solution.py:78
  11.8 0.8 copy-done.3
  12.6 1.5 %fusion.23 = f32[16,64,64]{2,1,0:T(8,128)} fusion(bf16[256,16,64]{0,2,1:T(8,128)(2,1)S(1)} %bitcast.77, f32[256,16]{0,1:T(8,128)S(1)} %get-tuple-element.159, bf16[256,2176]{0,1:T(8,128)(2,1)S(1)} %convolution_convert_fusion), kind=kOutput, calls=%fused_computation.37 | convolution fusion | flops 201850880 | bytes 835584 | tf_op jit(solution)/shard_map/jh,jhp,jn->hpn/dot_general | solution.py:90
  14.1 3.1 %collective-permute-start = (bf16[1,64,512]{2,1,0:T(8,128)(2,1)S(1)}, bf16[1,64,512]{2,1,0:T(8,128)(2,1)S(1)}, u32[]{:S(2)}, u32[]{:S(2)}) collective-permute-start(bf16[1,64,512]{2,1,0:T(8,128)(2,1)S(1)} %copy-done.6), channel_id=1, source_target_pairs={{0,1},{1,2},{2,3},{3,0},{4,5},{5,6},{6,7},{7,4},{8,9},{9,10},{10,1... | collective-permute-start | bytes 196616 | tf_op jit(solution)/shard_map/ppermute | solution.py:63
  17.2 0.9 fusion.46
  18.1 0.6 iota_compare_fusion
  18.7 0.6 iota_multiply_fusion
  19.3 1.3 %convert_reduce_fusion = (s32[4]{0:T(128)}, s32[4]{0:T(128)S(1)}) fusion(s32[256]{0:T(256)S(1)} %copy-done.1, s32[4]{0:T(128)} %get-tuple-element.167, s32[4]{0:T(128)S(1)} %get-tuple-element.166), kind=kLoop, calls=%fused_computation.84 | loop fusion | flops 6136 | bytes 1088 | tf_op jit(solution)/shard_map/reduce_sum | solution.py:110
  20.7 0.6 dynamic_slice.31
  21.3 0.7 fusion.50
  22.0 0.6 sub.64
  22.6 5.5 %fusion.11 = f32[256,16,64]{0,2,1:T(8,128)} fusion(bf16[256,16,64]{0,2,1:T(8,128)(2,1)} %bitcast.78, f32[256,256]{1,0:T(8,128)} %fusion.46, f32[16,256]{1,0:T(8,128)} %get-tuple-element.161, pred[256,256]{1,0:T(8,128)(4,1)} %iota_compare_fusion), kind=kOutput, calls=%fused_computation.15 | convolution fusion | flops 808452096 | bytes 1916928 | tf_op jit(solution)/shard_map/hij,jhp->ihp/dot_general | solution.py:88
  28.1 1.3 %gather_fusion = s32[128]{0:T(128)S(1)} fusion(s32[256]{0:T(256)S(1)} %copy-done.1, s32[1024]{0:T(1024)S(1)} %pad_clamp_fusion), kind=kCustom, calls=%fused_computation | custom fusion | bytes 1536 | tf_op jit(solution)/shard_map/gather | solution.py:115
  29.4 1.6 %collective-permute-start.1 = (bf16[1,64,512]{2,1,0:T(8,128)(2,1)S(1)}, bf16[1,64,512]{2,1,0:T(8,128)(2,1)S(1)}, u32[]{:S(2)}, u32[]{:S(2)}) collective-permute-start(bf16[1,64,512]{2,1,0:T(8,128)(2,1)S(1)} %collective-permute-done), channel_id=1, source_target_pairs={{0,1},{1,2},{2,3},{3,0},{4,5},{5,6},{6,7},{7,4},{8,9},{9,10},{10,1... | collective-permute-start | bytes 196616 | tf_op jit(solution)/shard_map/ppermute | solution.py:63
  31.1 1.3 %dynamic_slice.32 = s32[1]{0:T(128)} dynamic-slice(s32[4]{0:T(128)} %copy-done.11, s32[]{:T(128)S(6)} %select_n.62), dynamic_slice_sizes={1} | dynamic-slice | bytes 12 | tf_op jit(solution)/shard_map/dynamic_slice | solution.py:114
  32.4 10.2 %all-gather.1 = f32[4,1,16]{2,1,0:T(1,128)S(1)} all-gather(f32[1,1,16]{2,1,0:T(1,128)S(1)} %bitcast.82), channel_id=1, replica_groups=mesh['grp'=8,'seq'=4] {'seq'}, dimensions={0}, use_global_device_ids=true | all-gather | bytes 320 | tf_op jit(solution)/shard_map/all_gather | solution.py:9
  42.6 0.7 iota_compare_fusion.3
  43.3 6.9 %collective-permute-done.2 = bf16[1,64,512]{2,1,0:T(8,128)(2,1)S(1)} collective-permute-done((bf16[1,64,512]{2,1,0:T(8,128)(2,1)S(1)}, bf16[1,64,512]{2,1,0:T(8,128)(2,1)S(1)}, u32[]{:S(2)}, u32[]{:S(2)}) %collective-permute-start.2) | collective-permute-done | bytes 65568 | tf_op jit(solution)/shard_map/ppermute | solution.py:63
  50.2 0.6 constant_dynamic-update-slice_fusion.7
  50.8 0.6 constant_dynamic-update-slice_fusion.6
  51.4 0.6 constant_dynamic-update-slice_fusion.5
  52.0 0.6 constant_dynamic-update-slice_fusion.4
  52.7 0.6 constant_dynamic-update-slice_fusion.3
  53.3 0.6 constant_dynamic-update-slice_fusion.2
  53.9 0.6 constant_dynamic-update-slice_fusion.1
  54.5 0.6 constant_dynamic-update-slice_fusion
  55.1 10.3 %all-gather.4.cloned.1.call-done = f32[64,64,64]{2,1,0:T(8,128)} async-done(((f32[16,64,64]{2,1,0:T(8,128)}), f32[64,64,64]{2,1,0:T(8,128)}) %all-gather.4.cloned.1.call-update) | async-done | bytes 1048592 | tf_op jit(solution)/shard_map/all_gather | solution.py:9
  65.4 3.6 %while.18 = (s32[]{:T(128)}, f32[16,64,64]{2,1,0:T(8,128)S(1)}, s32[]{:T(128)}, f32[4,16]{1,0:T(4,128)S(1)}, f32[4,16,64,64]{3,2,1,0:T(8,128)}, /*index=5*/s32[]{:T(128)}, s32[]{:T(128)}) while((s32[]{:T(128)}, f32[16,64,64]{2,1,0:T(8,128)S(1)}, s32[]{:T(128)}, f32[4,16]{1,0:T(4,128)S(1)}, f32[4,16,64,64]{3,2,1,0:T(8,128)}, ...), condition=%wide.region_3.4_spmd.clone, body=%wide.region_2.3_spmd.clone.sunk | while | flops 262148 | bytes 786729 | solution.py:18
  65.4 1.2 %fusion.68 = f32[16,64,64]{2,1,0:T(8,128)S(1)} fusion(f32[4,16,64,64]{3,2,1,0:T(8,128)} %get-tuple-element.217, s32[]{:T(128)} %get-tuple-element.206, f32[16,64,64]{2,1,0:T(8,128)S(1)} %get-tuple-element.207, f32[16]{0:T(128)S(1)} %dynamic-slice_bitcast_fusion.2, pred[]{:T(512)S(6)} %compare.4, pred[]{:T(512)S(6)} %lt.134), kind=kLoop, calls=%fused_computation.2.clone.1 | loop fusion | flops 262144 | bytes 786502 | tf_op jit(solution)/shard_map/while/body/eval_jaxpr/jit(_where)/select_n | solution.py:16
  66.6 1.2 %fusion.68 = f32[16,64,64]{2,1,0:T(8,128)S(1)} fusion(f32[4,16,64,64]{3,2,1,0:T(8,128)} %get-tuple-element.217, s32[]{:T(128)} %get-tuple-element.206, f32[16,64,64]{2,1,0:T(8,128)S(1)} %get-tuple-element.207, f32[16]{0:T(128)S(1)} %dynamic-slice_bitcast_fusion.2, pred[]{:T(512)S(6)} %compare.4, pred[]{:T(512)S(6)} %lt.134), kind=kLoop, calls=%fused_computation.2.clone.1 | loop fusion | flops 262144 | bytes 786502 | tf_op jit(solution)/shard_map/while/body/eval_jaxpr/jit(_where)/select_n | solution.py:16
  67.9 1.2 %fusion.68 = f32[16,64,64]{2,1,0:T(8,128)S(1)} fusion(f32[4,16,64,64]{3,2,1,0:T(8,128)} %get-tuple-element.217, s32[]{:T(128)} %get-tuple-element.206, f32[16,64,64]{2,1,0:T(8,128)S(1)} %get-tuple-element.207, f32[16]{0:T(128)S(1)} %dynamic-slice_bitcast_fusion.2, pred[]{:T(512)S(6)} %compare.4, pred[]{:T(512)S(6)} %lt.134), kind=kLoop, calls=%fused_computation.2.clone.1 | loop fusion | flops 262144 | bytes 786502 | tf_op jit(solution)/shard_map/while/body/eval_jaxpr/jit(_where)/select_n | solution.py:16
  69.1 2.4 %fusion.15 = f32[256,16,64]{0,2,1:T(8,128)S(1)} fusion(f32[256,16,64]{0,2,1:T(8,128)} %fusion.11, f32[16,64,64]{2,1,0:T(8,128)S(1)} %get-tuple-element.123, f32[256,16]{0,1:T(8,128)S(1)} %copy-done.8, f32[256,64]{0,1:T(8,128)S(1)} %slice_convert_fusion), kind=kOutput, calls=%fused_computation.19 | convolution fusion | flops 201850880 | bytes 2441216 | tf_op jit(solution)/shard_map/ih,in,hpn->ihp/dot_general | solution.py:98
  71.5 1.4 %multiply_reduce_fusion = (f32[256]{0:T(256)S(1)}, f32[256,1024]{0,1:T(8,128)S(1)}) fusion(bf16[256,2176]{0,1:T(8,128)(2,1)} %copy-done.2, f32[256,16,64]{0,2,1:T(8,128)S(1)} %fusion.15), kind=kLoop, calls=%fused_computation.36 | loop fusion | flops 2096896 | bytes 2622464 | tf_op jit(solution)/shard_map/reduce_sum | solution.py:22
  73.0 0.8 fusion.16
  74.2 15.6 %all_gather.16 = bf16[512,512]{1,0:T(8,128)(2,1)S(1)} all-gather(bf16[128,512]{1,0:T(8,128)(2,1)S(1)} %multiply_convert_fusion.2), channel_id=1, replica_groups=mesh['grp'=8,'seq'=4] {'seq'}, dimensions={0}, use_global_device_ids=true | all-gather | bytes 655360 | tf_op jit(solution)/shard_map/all_gather | solution.py:121
  89.8 0.3 convolution_convert_fusion.1
  90.1 0.5 fusion.54
  91.1 0.5 broadcast.143
  91.6 0.7 reduce.6
  92.4 0.8 reshape.183
  93.2 3.3 %all-to-all-start = ((bf16[4,2,4096]{2,1,0:T(2,128)(2,1)}), bf16[4,2,4096]{2,1,0:T(2,128)(2,1)S(1)}, u32[]{:S(2)}, u32[]{:S(2)}) async-start(bf16[4,2,4096]{2,1,0:T(2,128)(2,1)} %reshape.183), calls=%async_computation | async-start | bytes 131072 | tf_op jit(solution)/shard_map/all_to_all | solution.py:127
  96.5 1.0 constant_dynamic-slice_fusion
  97.5 4.7 %all-to-all-done = bf16[4,2,4096]{2,1,0:T(2,128)(2,1)S(1)} async-done(((bf16[4,2,4096]{2,1,0:T(2,128)(2,1)}), bf16[4,2,4096]{2,1,0:T(2,128)(2,1)S(1)}, u32[]{:S(2)}, u32[]{:S(2)}) %all-to-all-start) | async-done | bytes 65568 | tf_op jit(solution)/shard_map/all_to_all | solution.py:127
  102.7 1.2 %fusion.17 = bf16[256,512]{1,0:T(8,128)(2,1)} fusion(f32[128,512]{1,0:T(8,128)S(1)} %fusion.55, bf16[256,512]{1,0:T(8,128)(2,1)S(1)} %fusion.16, s32[128]{0:T(128)S(1)} %broadcast_subtract_fusion, pred[128]{0:T(512)(128)(4,1)S(1)} %iota_compare_fusion.3), kind=kOutput, calls=%fused_computation.25 | convolution fusion | flops 201785344 | bytes 787072 | tf_op jit(solution)/shard_map/dot_general | solution.py:133
  (54 shorter events, 2.2 us)
Async XLA Ops:
  6.5 3.2 %copy-start = (bf16[512,2176]{1,0:T(8,128)(2,1)S(1)}, bf16[512,2176]{1,0:T(8,128)(2,1)}, u32[]{:S(2)}) copy-start(bf16[512,2176]{1,0:T(8,128)(2,1)} %param.14) | copy-start | bytes 6684676
  6.5 58.9 %all-gather.4.cloned.1.call-start = ((), (), s32[]{:S(2)}) async-start(), calls=%async_computation.1 | async-start | bytes 2621440 | tf_op jit(solution)/shard_map/all_gather | solution.py:9
  11.7 16.4 %copy-start.2 = (bf16[256,2176]{0,1:T(8,128)(2,1)}, bf16[256,2176]{0,1:T(8,128)(2,1)S(1)}, u32[]{:S(2)}) copy-start(bf16[256,2176]{0,1:T(8,128)(2,1)S(1)} %convolution_convert_fusion) | copy-start | bytes 3342340
  11.7 2.4 %copy-start.6 = (bf16[1,64,512]{2,1,0:T(8,128)(2,1)S(1)}, bf16[1,64,512]{2,1,0:T(8,128)(2,1)}, u32[]{:S(2)}) copy-start(bf16[1,64,512]{2,1,0:T(8,128)(2,1)} %param.19) | copy-start | bytes 196612
  11.7 7.6 %copy-start.1 = (s32[256]{0:T(256)S(1)}, s32[256]{0:T(256)}, u32[]{:S(2)}) copy-start(s32[256]{0:T(256)} %param.12) | copy-start | bytes 3076
  11.8 0.8 copy-start.3
  14.1 15.4 %collective-permute-start = (bf16[1,64,512]{2,1,0:T(8,128)(2,1)S(1)}, bf16[1,64,512]{2,1,0:T(8,128)(2,1)S(1)}, u32[]{:S(2)}, u32[]{:S(2)}) collective-permute-start(bf16[1,64,512]{2,1,0:T(8,128)(2,1)S(1)} %copy-done.6), channel_id=1, source_target_pairs={{0,1},{1,2},{2,3},{3,0},{4,5},{5,6},{6,7},{7,4},{8,9},{9,10},{10,1... | collective-permute-start | bytes 196616 | tf_op jit(solution)/shard_map/ppermute | solution.py:63
  22.6 5.5 %copy-start.11 = (s32[4]{0:T(128)}, s32[4]{0:T(128)S(1)}, u32[]{:S(2)}) copy-start(s32[4]{0:T(128)S(1)} %sub.64) | copy-start | bytes 52
  29.4 13.1 %collective-permute-start.1 = (bf16[1,64,512]{2,1,0:T(8,128)(2,1)S(1)}, bf16[1,64,512]{2,1,0:T(8,128)(2,1)S(1)}, u32[]{:S(2)}, u32[]{:S(2)}) collective-permute-start(bf16[1,64,512]{2,1,0:T(8,128)(2,1)S(1)} %collective-permute-done), channel_id=1, source_target_pairs={{0,1},{1,2},{2,3},{3,0},{4,5},{5,6},{6,7},{7,4},{8,9},{9,10},{10,1... | collective-permute-start | bytes 196616 | tf_op jit(solution)/shard_map/ppermute | solution.py:63
  42.6 7.6 %collective-permute-start.2 = (bf16[1,64,512]{2,1,0:T(8,128)(2,1)S(1)}, bf16[1,64,512]{2,1,0:T(8,128)(2,1)S(1)}, u32[]{:S(2)}, u32[]{:S(2)}) collective-permute-start(bf16[1,64,512]{2,1,0:T(8,128)(2,1)S(1)} %collective-permute-done.1), channel_id=1, source_target_pairs={{0,1},{1,2},{2,3},{3,0},{4,5},{5,6},{6,7},{7,4},{8,9},{9,10},{10,1... | collective-permute-start | bytes 196616 | tf_op jit(solution)/shard_map/ppermute | solution.py:63
  65.4 3.6 %copy-start.8 = (f32[256,16]{0,1:T(8,128)S(1)}, f32[256,16]{0,1:T(8,128)}, u32[]{:S(2)}) copy-start(f32[256,16]{0,1:T(8,128)} %get-tuple-element.158) | copy-start | bytes 49156
  69.1 3.9 %copy-start.4 = (bf16[256,512]{1,0:T(8,128)(2,1)S(1)}, bf16[256,512]{1,0:T(8,128)(2,1)}, u32[]{:S(2)}) copy-start(bf16[256,512]{1,0:T(8,128)(2,1)} %param.11) | copy-start | bytes 786436
  69.1 3.9 %copy-start.5 = (bf16[1024,512]{1,0:T(8,128)(2,1)S(1)}, bf16[1024,512]{1,0:T(8,128)(2,1)}, u32[]{:S(2)}) copy-start(bf16[1024,512]{1,0:T(8,128)(2,1)} %param.16) | copy-start | bytes 3145732
  69.1 3.9 %copy-start.9 = (f32[1024]{0:T(1024)S(1)}, f32[1024]{0:T(1024)}, u32[]{:S(2)}) copy-start(f32[1024]{0:T(1024)} %param.15) | copy-start | bytes 12292
  72.9 1.2 %copy-start.10 = (f32[512]{0:T(512)S(1)}, f32[512]{0:T(512)}, u32[]{:S(2)}) copy-start(f32[512]{0:T(512)} %param.17) | copy-start | bytes 6148
  72.9 16.9 %copy-start.7 = (bf16[1,512,192]{1,2,0:T(8,128)(2,1)S(1)}, bf16[1,512,192]{1,2,0:T(8,128)(2,1)}, u32[]{:S(2)}) copy-start(bf16[1,512,192]{1,2,0:T(8,128)(2,1)} %param.18) | copy-start | bytes 589828
  93.2 9.0 %all-to-all-start = ((bf16[4,2,4096]{2,1,0:T(2,128)(2,1)}), bf16[4,2,4096]{2,1,0:T(2,128)(2,1)S(1)}, u32[]{:S(2)}, u32[]{:S(2)}) async-start(bf16[4,2,4096]{2,1,0:T(2,128)(2,1)} %reshape.183), calls=%async_computation | async-start | bytes 131072 | tf_op jit(solution)/shard_map/all_to_all | solution.py:127
Sparse Core Ops, SparseCore 0:
  14.2 51.2 all-gather.3
